TPU v7x, 512 devices: a whole 4x8x8 slice. The times are simulated.
512 devices in a mesh: blk: 8 (over y_lo, core), team: 64 (over y_hi, x, z).
Axes of the slice: x: 4, y: 8 (y_hi: 2, y_lo: 4; y = y_hi * 4 + y_lo), z: 8, core: 2. Of those that a mesh axis runs over, the one named last changes fastest.
Arguments:
- features: bfloat16 [65536, 256], P(('blk', 'team')), may hold values from -6 to 6
- weight: bfloat16 [256, 256], replicated, may hold values from -0.375 to 0.375
- bias: float32 [256], replicated, may hold values from -3 to 3
- cotangent: bfloat16 [65536, 256], P(('blk', 'team')), may hold values from -6 to 6
- adj_cols: int32 [64, 8, 8, 12], P('team', None, 'blk'), may hold values from 0 to 63, as said below
- adj_vals: bfloat16 [64, 8, 8, 12, 128, 128], P('team', None, 'blk'), as said below
Outputs:
- hidden: bfloat16 [65536, 256], P(('blk', 'team'))
- grad_input: bfloat16 [65536, 256], P(('blk', 'team'))
- grad_weight: float32 [256, 256], replicated
- grad_bias: float32 [256], replicated
Inputs may be any that keep to these rules, and one draw needn't show every extreme that they name: `adj_cols`: for every node panel and column group the 12 entries are distinct. Block (i, j) of A is listed exactly when block (j, i) is, every column panel is listed by exactly 12 row panels of each column group, and A is symmetric. `adj_vals`: the block listed for panels (i, j) is the transpose of the block listed for (j, i), so A is symmetric.
All inputs are finite; a program needn't handle non-finite values.
Results may differ from a plain program's by a relative error of at most 0.0075.
Values may be sent and summed in bfloat16 or wider, within the bound.
No kernel may reach another device: no remote copies, remote signals or barrier semaphores. Data moves between devices by JAX's collectives and lax.ppermute only.
A program may use at most 64 MiB of HBM per device.

v0:
```python
import jax
import jax.numpy as jnp
from jax import lax
from jax.sharding import Mesh
from jax.sharding import PartitionSpec as P

BLK_AXES = ("y_lo", "core")
TEAM_AXES = ("y_hi", "x", "z")
PLANE = ("x", "z")
ALL_AXES = BLK_AXES + TEAM_AXES


def fine_mesh(mesh):
    blk = mesh.shape["blk"]
    team = mesh.shape["team"]
    sizes = (blk // 2, 2, 2, 4, team // 8)
    return Mesh(mesh.devices.reshape(sizes), ALL_AXES)


def gather_team(rows):
    other = lax.ppermute(rows, "y_hi", perm=[(0, 1), (1, 0)])
    pair = jnp.stack([rows, other], axis=0)
    full = lax.all_gather(pair, PLANE, axis=0, tiled=True)
    return full.reshape(-1, rows.shape[1])


def member_slots(members, plane_size):
    my_hi = lax.axis_index("y_hi")
    return members % plane_size * 2 + (members // plane_size != my_hi).astype(jnp.int32)


def collect(panels, slots, adj_vals):
    block = adj_vals.shape[-1]
    width = panels.shape[1]
    stacked = panels.reshape(panels.shape[0] // block, block, width)
    picked = jnp.take(stacked, slots, axis=0)
    summed = jnp.einsum(
        "rkij,rkjf->rif", adj_vals[0, :, 0], picked, preferred_element_type=jnp.float32
    )
    return summed.reshape(-1, width)


def activation(value):
    return jax.nn.gelu(value, approximate=True)


def local(features, weight, bias, cotangent, adj_cols, adj_vals):
    plane_size = lax.psum(1, PLANE)
    slots = member_slots(adj_cols[0, :, 0, :], plane_size)
    product = jnp.dot(features, weight, preferred_element_type=jnp.float32).astype(jnp.bfloat16)
    gathered = gather_team(product)
    partial_rows = collect(gathered, slots, adj_vals)
    summed = lax.psum_scatter(partial_rows, BLK_AXES, scatter_dimension=0, tiled=True)
    pre = summed + bias[None, :]
    activated, pullback = jax.vjp(activation, pre)
    hidden = activated.astype(jnp.bfloat16)
    pulled = pullback(cotangent.astype(jnp.float32))[0].astype(jnp.bfloat16)
    pulled_group = gather_team(pulled)
    partial_back = collect(pulled_group, slots, adj_vals)
    spread = lax.psum_scatter(partial_back, BLK_AXES, scatter_dimension=0, tiled=True).astype(
        jnp.bfloat16
    )
    grad_input = jnp.dot(spread, weight.T, preferred_element_type=jnp.float32).astype(jnp.bfloat16)
    local_weight = lax.dot_general(
        features, spread, (((0,), (0,)), ((), ())), preferred_element_type=jnp.float32
    )
    local_bias = jnp.sum(pulled.astype(jnp.float32), axis=0)
    both = jnp.concatenate([local_weight, local_bias[None, :]], axis=0)
    both = lax.psum(both, PLANE)
    both = lax.psum(both, ("y_lo", "y_hi", "core"))
    grad_weight = both[:-1]
    grad_bias = both[-1]
    return (hidden, grad_input, grad_weight, grad_bias)


def solution(mesh):
    fine = fine_mesh(mesh)
    rows = P(ALL_AXES, None)
    return jax.shard_map(
        local,
        mesh=fine,
        in_specs=(
            rows,
            P(),
            P(),
            rows,
            P(TEAM_AXES, None, BLK_AXES, None),
            P(TEAM_AXES, None, BLK_AXES, None, None, None),
        ),
        out_specs=(rows, rows, P(), P()),
        check_vma=False,
    )
```

profile of v0, /device:TPU:1, one launch (start us, length us, event | category | flops | bytes accessed | tf_op | source)
XLA Modules:
  0.0 590.6 jit_solution(9726838023997011577)
XLA Ops:
  7.2 0.0 copy-start
  7.2 0.0 all-gather.3.cloned.1.call-start
  7.2 1.2 convolution_convert_fusion.1
  8.5 8.3 %collective-permute-start = (bf16[128,256]{1,0:T(8,128)(2,1)S(1)}, bf16[128,256]{1,0:T(8,128)(2,1)S(1)}, u32[]{:S(2)}, u32[]{:S(2)}) collective-permute-start(bf16[128,256]{1,0:T(8,128)(2,1)S(1)} %convolution_convert_fusion.1), channel_id=1, source_target_pairs={{0,32},{32,0},{1,33},{33,1},{2,34},{34,2},{3,35},{35,3},{4,36},{36... | collective-permute-start | bytes 196616 | tf_op jit(solution)/shard_map/ppermute | solution.py:21
  16.8 1.7 collective-permute-done
  18.5 0.7 pad_maximum_fusion.1
  19.1 0.0 all-gather.3.cloned.1.call-update
  19.2 0.0 reduce-scatter.3.cloned.1.call-start
  19.2 0.7 compare_and_fusion
  19.9 0.1 reshape.42
  20.0 91.1 %all-gather.3.cloned.1.call-done = bf16[64,128,256]{2,1,0:T(8,128)(2,1)} async-done(((bf16[2,128,256]{2,1,0:T(8,128)(2,1)}), bf16[64,128,256]{2,1,0:T(8,128)(2,1)}) %all-gather.3.cloned.1.call-update) | async-done | bytes 4194320 | tf_op jit(solution)/shard_map/all_gather | solution.py:23
  111.1 8.2 %gather_fusion = bf16[96,128,256]{2,1,0:T(8,128)(2,1)} fusion(bf16[64,128,256]{2,1,0:T(8,128)(2,1)} %all-gather.3.cloned.1.call-done, s32[1024]{0:T(1024)S(1)} %pad_clamp_fusion), kind=kCustom, calls=%fused_computation.clone | custom fusion | bytes 12583296 | tf_op jit(solution)/shard_map/jit(_take)/gather | solution.py:36
  119.3 0.0 copy-done
  119.3 0.0 copy-start.3
  119.3 0.0 copy-start.4
  119.3 5.2 fusion.2
  124.5 0.0 reduce-scatter.3.cloned.1.call-update
  124.5 0.0 all-gather.5.cloned.1.call-start
  124.6 38.0 %reduce-scatter.3.cloned.1.call-done = f32[128,256]{1,0:T(8,128)} async-done(((f32[1024,256]{1,0:T(8,128)}), f32[128,256]{1,0:T(8,128)}) %reduce-scatter.3.cloned.1.call-update) | async-done | bytes 131088 | tf_op jit(solution)/shard_map/reduce_scatter | solution.py:53
  162.5 0.0 copy-done.3
  162.5 0.0 copy-done.4
  162.5 1.6 convert_reduce_fusion
  164.2 5.5 collective-permute-start.1
  169.6 3.7 collective-permute-done.1
  173.3 0.7 pad_maximum_fusion.2
  174.0 0.0 all-gather.5.cloned.1.call-update
  174.0 0.0 reduce-scatter.5.cloned.1.call-start
  174.1 86.9 %all-gather.5.cloned.1.call-done = bf16[64,128,256]{2,1,0:T(8,128)(2,1)} async-done(((bf16[2,128,256]{2,1,0:T(8,128)(2,1)}), bf16[64,128,256]{2,1,0:T(8,128)(2,1)}) %all-gather.5.cloned.1.call-update) | async-done | bytes 4194320 | tf_op jit(solution)/shard_map/all_gather | solution.py:23
  260.9 8.2 %gather_fusion.1 = bf16[96,128,256]{2,1,0:T(8,128)(2,1)} fusion(bf16[64,128,256]{2,1,0:T(8,128)(2,1)} %all-gather.5.cloned.1.call-done, s32[1024]{0:T(1024)S(1)} %pad_clamp_fusion), kind=kCustom, calls=%fused_computation.1.clone | custom fusion | bytes 12583296 | tf_op jit(solution)/shard_map/jit(_take)/gather | solution.py:36
  269.1 0.0 copy-start.2
  269.1 0.0 copy-start.1
  269.1 5.2 fusion
  274.3 0.0 reduce-scatter.5.cloned.1.call-update
  274.3 0.0 all-reduce.3.cloned.1.call-start
  274.4 38.0 %reduce-scatter.5.cloned.1.call-done = f32[128,256]{1,0:T(8,128)} async-done(((f32[1024,256]{1,0:T(8,128)}), f32[128,256]{1,0:T(8,128)}) %reduce-scatter.5.cloned.1.call-update) | async-done | bytes 131088 | tf_op jit(solution)/shard_map/reduce_scatter | solution.py:60
  312.3 0.0 copy-done.2
  312.3 1.1 convolution_bitcast_fusion
  313.5 0.7 pad_maximum_fusion
  314.2 0.0 all-reduce.3.cloned.1.call-update
  314.2 0.0 all-reduce.5.cloned.1.call-start
  314.3 153.2 %all-reduce.3.cloned.1.call-done = f32[257,256]{1,0:T(8,128)} async-done(((f32[257,256]{1,0:T(8,128)}), f32[257,256]{1,0:T(8,128)}) %all-reduce.3.cloned.1.call-update) | async-done | bytes 263184 | tf_op jit(solution)/shard_map/psum | solution.py:69
  467.4 0.0 all-reduce.5.cloned.1.call-update
  467.5 0.0 copy-done.1
  467.5 1.7 convolution_convert_fusion
  469.2 111.6 %all-reduce.5.cloned.1.call-done = f32[257,256]{1,0:T(8,128)} async-done(((f32[257,256]{1,0:T(8,128)}), f32[257,256]{1,0:T(8,128)}) %all-reduce.5.cloned.1.call-update) | async-done | bytes 263184 | tf_op jit(solution)/shard_map/psum | solution.py:70
  580.8 1.3 slice.13
  582.1 1.7 slice.12
  (1 shorter events, 0.0 us)
Async XLA Ops:
  7.2 112.1 %copy-start = (bf16[1,8,1,12,128,128]{5,4,3,2,1,0:T(8,128)(2,1)S(1)}, bf16[1,8,1,12,128,128]{5,4,3,2,1,0:T(8,128)(2,1)}, u32[]{:S(2)}) copy-start(bf16[1,8,1,12,128,128]{5,4,3,2,1,0:T(8,128)(2,1)} %param.13) | copy-start | bytes 9437188
  7.2 103.9 %all-gather.3.cloned.1.call-start = ((), (), s32[]{:S(2)}) async-start(), calls=%async_computation.2 | async-start | bytes 4325376 | tf_op jit(solution)/shard_map/all_gather | solution.py:23
  8.5 10.0 %collective-permute-start = (bf16[128,256]{1,0:T(8,128)(2,1)S(1)}, bf16[128,256]{1,0:T(8,128)(2,1)S(1)}, u32[]{:S(2)}, u32[]{:S(2)}) collective-permute-start(bf16[128,256]{1,0:T(8,128)(2,1)S(1)} %convolution_convert_fusion.1), channel_id=1, source_target_pairs={{0,32},{32,0},{1,33},{33,1},{2,34},{34,2},{3,35},{35,3},{4,36},{36... | collective-permute-start | bytes 196616 | tf_op jit(solution)/shard_map/ppermute | solution.py:21
  19.2 143.4 %reduce-scatter.3.cloned.1.call-start = ((), (), s32[]{:S(2)}) async-start(), calls=%async_computation.3 | async-start | bytes 1179648 | tf_op jit(solution)/shard_map/reduce_scatter | solution.py:53
  119.3 43.2 %copy-start.3 = (bf16[128,256]{1,0:T(8,128)(2,1)S(1)}, bf16[128,256]{1,0:T(8,128)(2,1)}, u32[]{:S(2)}) copy-start(bf16[128,256]{1,0:T(8,128)(2,1)} %param.11) | copy-start | bytes 196612
  119.3 43.2 %copy-start.4 = (f32[256]{0:T(256)S(1)}, f32[256]{0:T(256)}, u32[]{:S(2)}) copy-start(f32[256]{0:T(256)} %param.10) | copy-start | bytes 3076
  124.5 136.4 %all-gather.5.cloned.1.call-start = ((), (), s32[]{:S(2)}) async-start(), calls=%async_computation.4 | async-start | bytes 4325376 | tf_op jit(solution)/shard_map/all_gather | solution.py:23
  164.2 9.1 %collective-permute-start.1 = (bf16[128,256]{1,0:T(8,128)(2,1)S(1)}, bf16[128,256]{1,0:T(8,128)(2,1)S(1)}, u32[]{:S(2)}, u32[]{:S(2)}) collective-permute-start(bf16[128,256]{1,0:T(8,128)(2,1)S(1)} %get-tuple-element.6), channel_id=1, source_target_pairs={{0,32},{32,0},{1,33},{33,1},{2,34},{34,2},{3,35},{35,3},{4,36},{36... | collective-permute-start | bytes 196616 | tf_op jit(solution)/shard_map/ppermute | solution.py:21
  174.0 138.3 %reduce-scatter.5.cloned.1.call-start = ((), (), s32[]{:S(2)}) async-start(), calls=%async_computation.5 | async-start | bytes 1179648 | tf_op jit(solution)/shard_map/reduce_scatter | solution.py:60
  269.1 43.2 %copy-start.2 = (bf16[128,256]{1,0:T(8,128)(2,1)S(1)}, bf16[128,256]{1,0:T(8,128)(2,1)}, u32[]{:S(2)}) copy-start(bf16[128,256]{1,0:T(8,128)(2,1)} %param.8) | copy-start | bytes 196612
  269.1 198.3 %copy-start.1 = (bf16[256,256]{1,0:T(8,128)(2,1)S(1)}, bf16[256,256]{1,0:T(8,128)(2,1)}, u32[]{:S(2)}) copy-start(bf16[256,256]{1,0:T(8,128)(2,1)} %param.9) | copy-start | bytes 393220
  274.3 193.1 %all-reduce.3.cloned.1.call-start = ((), (), s32[]{:S(2)}) async-start(), calls=%async_computation.6 | async-start | bytes 540672 | tf_op jit(solution)/shard_map/psum | solution.py:69
  314.2 266.6 %all-reduce.5.cloned.1.call-start = ((), (), s32[]{:S(2)}) async-start(), calls=%async_computation.7 | async-start | bytes 540672 | tf_op jit(solution)/shard_map/psum | solution.py:70
Sparse Core Ops, SparseCore 0:
  19.3 91.7 all-gather.2
  124.6 37.8 reduce-scatter.2
  174.1 86.7 all-gather.4
  274.5 37.8 reduce-scatter.4
  315.6 151.7 all-reduce.2
  469.6 111.1 all-reduce.4
where the time goes:
time: 591 us
  waiting for transfers between devices  524 us (89%)
  local copies, waits for them, and re-layouts  19.4 us (3%)
  matrix products  14.5 us (2%)
  between operations  14.2 us (2%)
  starting transfers between devices  14 us (2%)
    all_gather x2, waiting for transfers between devices, gather_team(): full = lax.all_gather(pair, PLANE, axis=0, tiled=True)  178 us
    psum x1, waiting for transfers between devices, local(): both = lax.psum(both, PLANE)  153 us
    psum x1, waiting for transfers between devices, local(): both = lax.psum(both, ('y_lo', 'y_hi', 'core'))  112 us
    reduce_scatter x1, waiting for transfers between devices, local(): lax.psum_scatter(partial_back, BLK_AXES, scatter_dimension=0, tiled=True)  38 us
    reduce_scatter x1, waiting for transfers between devices, local(): lax.psum_scatter(partial_rows, BLK_AXES, scatter_dimension=0, tiled=True)  38 us
    gather x2, local copies, waits for them, and re-layouts, collect(): picked = jnp.take(stacked, slots, axis=0)  16.4 us
    ppermute x2, starting transfers between devices, gather_team(): other = lax.ppermute(rows, 'y_hi', perm=[(0, 1), (1, 0)])  13.7 us
  transfers between devices with their start and end apart: 8, of which 8 were waited for; matrix products, arithmetic and copies ran while one was open for 0% of the time, Pallas kernels for 0%

commit v1 on v0

--- a/solution.py
+++ b/solution.py
@@ -66,7 +66,7 @@
     )
     local_bias = jnp.sum(pulled.astype(jnp.float32), axis=0)
     both = jnp.concatenate([local_weight, local_bias[None, :]], axis=0)
-    both = lax.psum(both, PLANE)
+    both = lax.psum(lax.psum(both, "z"), "x")
     both = lax.psum(both, ("y_lo", "y_hi", "core"))
     grad_weight = both[:-1]
     grad_bias = both[-1]

time: 591 us -> 570 us (0.964)
  waiting for transfers between devices: 524 us -> 503 us
    psum x1 -> x2, waiting for transfers between devices: 153 us -> 130 us  [local(): both = lax.psum(lax.psum(both, 'z'), 'x')]
  transfers between devices with their start and end apart: 8 -> 9, of which waited for: 8 -> 9; matrix products, arithmetic and copies ran while one was open for 0% -> 0% of each run, Pallas kernels for 0% -> 0%
where the time goes in v1:
time: 570 us; the launch traced here: 569 us
  waiting for transfers between devices  503 us (88%)
  local copies, waits for them, and re-layouts  19.4 us (3%)
  matrix products  14.5 us (3%)
  between operations  14.2 us (2%)
  starting transfers between devices  14 us (2%)
    all_gather x2, waiting for transfers between devices, gather_team(): full = lax.all_gather(pair, PLANE, axis=0, tiled=True)  178 us
    psum x2, waiting for transfers between devices, local(): both = lax.psum(lax.psum(both, 'z'), 'x')  130 us
    psum x1, waiting for transfers between devices, local(): both = lax.psum(both, ('y_lo', 'y_hi', 'core'))  113 us
    reduce_scatter x1, waiting for transfers between devices, local(): lax.psum_scatter(partial_back, BLK_AXES, scatter_dimension=0, tiled=True)  38 us
    reduce_scatter x1, waiting for transfers between devices, local(): lax.psum_scatter(partial_rows, BLK_AXES, scatter_dimension=0, tiled=True)  38 us
    gather x2, local copies, waits for them, and re-layouts, collect(): picked = jnp.take(stacked, slots, axis=0)  16.4 us
    ppermute x2, starting transfers between devices, gather_team(): other = lax.ppermute(rows, 'y_hi', perm=[(0, 1), (1, 0)])  13.7 us
  transfers between devices with their start and end apart: 9, of which 9 were waited for; matrix products, arithmetic and copies ran while one was open for 0% of the time, Pallas kernels for 0%

profile of v1, /device:TPU:1, one launch (start us, length us, event | category | flops | bytes accessed | tf_op | source)
XLA Modules:
  0.0 569.4 jit_solution(75321327353494652)
XLA Ops:
  7.2 0.0 copy-start
  7.2 0.0 all-gather.3.cloned.1.call-start
  7.2 1.2 convolution_convert_fusion.1
  8.5 8.3 %collective-permute-start = (bf16[128,256]{1,0:T(8,128)(2,1)S(1)}, bf16[128,256]{1,0:T(8,128)(2,1)S(1)}, u32[]{:S(2)}, u32[]{:S(2)}) collective-permute-start(bf16[128,256]{1,0:T(8,128)(2,1)S(1)} %convolution_convert_fusion.1), channel_id=1, source_target_pairs={{0,32},{32,0},{1,33},{33,1},{2,34},{34,2},{3,35},{35,3},{4,36},{36... | collective-permute-start | bytes 196616 | tf_op jit(solution)/shard_map/ppermute | solution.py:21
  16.8 1.7 collective-permute-done
  18.5 0.7 pad_maximum_fusion.1
  19.1 0.0 all-gather.3.cloned.1.call-update
  19.2 0.0 reduce-scatter.3.cloned.1.call-start
  19.2 0.7 compare_and_fusion
  19.9 0.1 reshape.42
  20.0 91.1 %all-gather.3.cloned.1.call-done = bf16[64,128,256]{2,1,0:T(8,128)(2,1)} async-done(((bf16[2,128,256]{2,1,0:T(8,128)(2,1)}), bf16[64,128,256]{2,1,0:T(8,128)(2,1)}) %all-gather.3.cloned.1.call-update) | async-done | bytes 4194320 | tf_op jit(solution)/shard_map/all_gather | solution.py:23
  111.1 8.2 %gather_fusion = bf16[96,128,256]{2,1,0:T(8,128)(2,1)} fusion(bf16[64,128,256]{2,1,0:T(8,128)(2,1)} %all-gather.3.cloned.1.call-done, s32[1024]{0:T(1024)S(1)} %pad_clamp_fusion), kind=kCustom, calls=%fused_computation.clone | custom fusion | bytes 12583296 | tf_op jit(solution)/shard_map/jit(_take)/gather | solution.py:36
  119.3 0.0 copy-done
  119.3 0.0 copy-start.3
  119.3 0.0 copy-start.4
  119.3 5.2 fusion.2
  124.5 0.0 reduce-scatter.3.cloned.1.call-update
  124.5 0.0 all-gather.5.cloned.1.call-start
  124.6 38.0 %reduce-scatter.3.cloned.1.call-done = f32[128,256]{1,0:T(8,128)} async-done(((f32[1024,256]{1,0:T(8,128)}), f32[128,256]{1,0:T(8,128)}) %reduce-scatter.3.cloned.1.call-update) | async-done | bytes 131088 | tf_op jit(solution)/shard_map/reduce_scatter | solution.py:53
  162.5 0.0 copy-done.3
  162.5 0.0 copy-done.4
  162.5 1.6 convert_reduce_fusion
  164.2 5.5 collective-permute-start.1
  169.6 3.7 collective-permute-done.1
  173.3 0.7 pad_maximum_fusion.2
  174.0 0.0 all-gather.5.cloned.1.call-update
  174.0 0.0 reduce-scatter.5.cloned.1.call-start
  174.1 86.9 %all-gather.5.cloned.1.call-done = bf16[64,128,256]{2,1,0:T(8,128)(2,1)} async-done(((bf16[2,128,256]{2,1,0:T(8,128)(2,1)}), bf16[64,128,256]{2,1,0:T(8,128)(2,1)}) %all-gather.5.cloned.1.call-update) | async-done | bytes 4194320 | tf_op jit(solution)/shard_map/all_gather | solution.py:23
  260.9 8.2 %gather_fusion.1 = bf16[96,128,256]{2,1,0:T(8,128)(2,1)} fusion(bf16[64,128,256]{2,1,0:T(8,128)(2,1)} %all-gather.5.cloned.1.call-done, s32[1024]{0:T(1024)S(1)} %pad_clamp_fusion), kind=kCustom, calls=%fused_computation.1.clone | custom fusion | bytes 12583296 | tf_op jit(solution)/shard_map/jit(_take)/gather | solution.py:36
  269.1 0.0 copy-start.2
  269.1 0.0 copy-start.1
  269.1 5.2 fusion
  274.3 0.0 reduce-scatter.5.cloned.1.call-update
  274.3 0.0 all-reduce.4.cloned.1.call-start
  274.4 38.0 %reduce-scatter.5.cloned.1.call-done = f32[128,256]{1,0:T(8,128)} async-done(((f32[1024,256]{1,0:T(8,128)}), f32[128,256]{1,0:T(8,128)}) %reduce-scatter.5.cloned.1.call-update) | async-done | bytes 131088 | tf_op jit(solution)/shard_map/reduce_scatter | solution.py:60
  312.3 0.0 copy-done.2
  312.3 1.1 convolution_bitcast_fusion
  313.5 0.7 pad_maximum_fusion
  314.2 0.0 all-reduce.4.cloned.1.call-update
  314.2 0.0 all-reduce.6.cloned.1.call-start
  314.3 75.7 %all-reduce.4.cloned.1.call-done = f32[257,256]{1,0:T(8,128)} async-done(((f32[257,256]{1,0:T(8,128)}), f32[257,256]{1,0:T(8,128)}) %all-reduce.4.cloned.1.call-update) | async-done | bytes 263184 | tf_op jit(solution)/shard_map/psum | solution.py:69
  389.9 0.0 all-reduce.6.cloned.1.call-update
  390.0 0.0 all-reduce.8.cloned.1.call-start
  390.0 54.8 %all-reduce.6.cloned.1.call-done = f32[257,256]{1,0:T(8,128)} async-done(((f32[257,256]{1,0:T(8,128)}), f32[257,256]{1,0:T(8,128)}) %all-reduce.6.cloned.1.call-update) | async-done | bytes 263184 | tf_op jit(solution)/shard_map/psum | solution.py:69
  444.8 0.0 all-reduce.8.cloned.1.call-update
  444.8 0.0 copy-done.1
  444.9 1.7 convolution_convert_fusion
  446.6 113.0 %all-reduce.8.cloned.1.call-done = f32[257,256]{1,0:T(8,128)} async-done(((f32[257,256]{1,0:T(8,128)}), f32[257,256]{1,0:T(8,128)}) %all-reduce.8.cloned.1.call-update) | async-done | bytes 263184 | tf_op jit(solution)/shard_map/psum | solution.py:70
  559.6 1.3 slice.13
  560.9 1.7 slice.12
  (1 shorter events, 0.0 us)
Async XLA Ops:
  7.2 112.1 %copy-start = (bf16[1,8,1,12,128,128]{5,4,3,2,1,0:T(8,128)(2,1)S(1)}, bf16[1,8,1,12,128,128]{5,4,3,2,1,0:T(8,128)(2,1)}, u32[]{:S(2)}) copy-start(bf16[1,8,1,12,128,128]{5,4,3,2,1,0:T(8,128)(2,1)} %param.13) | copy-start | bytes 9437188
  7.2 103.9 %all-gather.3.cloned.1.call-start = ((), (), s32[]{:S(2)}) async-start(), calls=%async_computation.2 | async-start | bytes 4325376 | tf_op jit(solution)/shard_map/all_gather | solution.py:23
  8.5 10.0 %collective-permute-start = (bf16[128,256]{1,0:T(8,128)(2,1)S(1)}, bf16[128,256]{1,0:T(8,128)(2,1)S(1)}, u32[]{:S(2)}, u32[]{:S(2)}) collective-permute-start(bf16[128,256]{1,0:T(8,128)(2,1)S(1)} %convolution_convert_fusion.1), channel_id=1, source_target_pairs={{0,32},{32,0},{1,33},{33,1},{2,34},{34,2},{3,35},{35,3},{4,36},{36... | collective-permute-start | bytes 196616 | tf_op jit(solution)/shard_map/ppermute | solution.py:21
  19.2 143.4 %reduce-scatter.3.cloned.1.call-start = ((), (), s32[]{:S(2)}) async-start(), calls=%async_computation.3 | async-start | bytes 1179648 | tf_op jit(solution)/shard_map/reduce_scatter | solution.py:53
  119.3 43.2 %copy-start.3 = (bf16[128,256]{1,0:T(8,128)(2,1)S(1)}, bf16[128,256]{1,0:T(8,128)(2,1)}, u32[]{:S(2)}) copy-start(bf16[128,256]{1,0:T(8,128)(2,1)} %param.11) | copy-start | bytes 196612
  119.3 43.2 %copy-start.4 = (f32[256]{0:T(256)S(1)}, f32[256]{0:T(256)}, u32[]{:S(2)}) copy-start(f32[256]{0:T(256)} %param.10) | copy-start | bytes 3076
  124.5 136.4 %all-gather.5.cloned.1.call-start = ((), (), s32[]{:S(2)}) async-start(), calls=%async_computation.4 | async-start | bytes 4325376 | tf_op jit(solution)/shard_map/all_gather | solution.py:23
  164.2 9.1 %collective-permute-start.1 = (bf16[128,256]{1,0:T(8,128)(2,1)S(1)}, bf16[128,256]{1,0:T(8,128)(2,1)S(1)}, u32[]{:S(2)}, u32[]{:S(2)}) collective-permute-start(bf16[128,256]{1,0:T(8,128)(2,1)S(1)} %get-tuple-element.6), channel_id=1, source_target_pairs={{0,32},{32,0},{1,33},{33,1},{2,34},{34,2},{3,35},{35,3},{4,36},{36... | collective-permute-start | bytes 196616 | tf_op jit(solution)/shard_map/ppermute | solution.py:21
  174.0 138.3 %reduce-scatter.5.cloned.1.call-start = ((), (), s32[]{:S(2)}) async-start(), calls=%async_computation.5 | async-start | bytes 1179648 | tf_op jit(solution)/shard_map/reduce_scatter | solution.py:60
  269.1 43.2 %copy-start.2 = (bf16[128,256]{1,0:T(8,128)(2,1)S(1)}, bf16[128,256]{1,0:T(8,128)(2,1)}, u32[]{:S(2)}) copy-start(bf16[128,256]{1,0:T(8,128)(2,1)} %param.8) | copy-start | bytes 196612
  269.1 175.7 %copy-start.1 = (bf16[256,256]{1,0:T(8,128)(2,1)S(1)}, bf16[256,256]{1,0:T(8,128)(2,1)}, u32[]{:S(2)}) copy-start(bf16[256,256]{1,0:T(8,128)(2,1)} %param.9) | copy-start | bytes 393220
  274.3 115.6 %all-reduce.4.cloned.1.call-start = ((), (), s32[]{:S(2)}) async-start(), calls=%async_computation.6 | async-start | bytes 540672 | tf_op jit(solution)/shard_map/psum | solution.py:69
  314.2 130.6 %all-reduce.6.cloned.1.call-start = ((), (), s32[]{:S(2)}) async-start(), calls=%async_computation.7 | async-start | bytes 540672 | tf_op jit(solution)/shard_map/psum | solution.py:69
  390.0 169.6 %all-reduce.8.cloned.1.call-start = ((), (), s32[]{:S(2)}) async-start(), calls=%async_computation.8 | async-start | bytes 540672 | tf_op jit(solution)/shard_map/psum | solution.py:70
Sparse Core Ops, SparseCore 0:
  19.3 91.7 all-gather.2
  124.6 37.8 reduce-scatter.2
  174.1 86.7 all-gather.4
  274.5 37.8 reduce-scatter.4
  314.5 75.3 all-reduce.3
  392.3 52.5 all-reduce.5
  447.3 112.2 all-reduce.7
